TPU v7x, 32 devices: a whole 2x2x4 slice. The times are simulated.
32 devices in a mesh: grp: 4 (over y, core), tm: 8 (over z, x).
Axes of the slice: x: 2, y: 2, z: 4, core: 2. Of those that a mesh axis runs over, the one named last changes fastest.
Arguments:
- wave: bfloat16 [4, 327680], P('grp', 'tm'), may hold values from -6 to 6
- assign: int32 [4, 1024], P('grp', 'tm'), may hold values from 0 to 16383
- w_first: bfloat16 [10, 512], replicated, may hold values from -2 to 2
- w_mid: bfloat16 [4, 1536, 512], replicated, may hold values from -0.15625 to 0.15625
- w_tail: bfloat16 [2, 1024, 512], replicated, may hold values from -0.1875 to 0.1875
- w_proj: bfloat16 [512, 768], replicated, may hold values from -0.25 to 0.25
- centroids: float32 [16384, 768], P('tm'), may hold values from -6 to 6
- prior: float32 [16384], P('tm'), may hold values from 1 to 16
Outputs:
- new_centroids: float32 [16384, 768], P('tm')
- new_counts: float32 [16384], P('tm')
- distortion: float32 [4, 1024], P('grp', 'tm')
All inputs are finite; a program needn't handle non-finite values.
Results may differ from a plain program's by a relative error of at most 0.007.
Values may be sent and summed in bfloat16 or wider, within the bound.
A program may use at most 128 MiB of HBM per device.

v0:
```python
import jax
import jax.numpy as jnp
from jax import lax
from jax.sharding import PartitionSpec as P

HALO = 80
EPS = 1e-05


def passed_along(value, axis, steps):
    count = lax.axis_size(axis)
    leading, last = (max(0, -steps), min(count, count - steps))
    return lax.ppermute(value, axis, [(source, source + steps) for source in range(leading, last)])


def norm_rows(accum):
    row_mean = jnp.mean(accum, axis=-1, keepdims=True)
    centred = accum - row_mean
    spread = jnp.mean(centred * centred, axis=-1, keepdims=True)
    return centred * lax.rsqrt(spread + EPS)


def activate(accum):
    return jax.nn.gelu(norm_rows(accum), approximate=False).astype(jnp.bfloat16)


def first_layer(samples, w_first):
    windows = samples.reshape(-1, 5)
    accum = jnp.dot(windows[:-1], w_first[:5], preferred_element_type=jnp.float32)
    accum = accum + jnp.dot(windows[1:], w_first[5:], preferred_element_type=jnp.float32)
    return activate(accum)


def odd_layer(inputs, weight):
    channels = inputs.shape[1]
    out_len = (inputs.shape[0] - 3) // 2 + 1
    paired = jnp.concatenate([inputs, jnp.zeros((1, channels), inputs.dtype)], axis=0).reshape(
        out_len + 1, 2 * channels
    )
    accum = jnp.dot(paired[:out_len], weight[: 2 * channels], preferred_element_type=jnp.float32)
    accum = accum + jnp.dot(
        paired[1:, :channels], weight[2 * channels :], preferred_element_type=jnp.float32
    )
    return activate(accum)


def even_layer(inputs, weight):
    channels = inputs.shape[1]
    paired = inputs.reshape(inputs.shape[0] // 2, 2 * channels)
    return activate(jnp.dot(paired, weight, preferred_element_type=jnp.float32))


def encode(samples, w_first, w_mid, w_tail):
    hidden = first_layer(samples, w_first)
    for layer_num in range(4):
        hidden = odd_layer(hidden, w_mid[layer_num])
    for layer_num in range(2):
        hidden = even_layer(hidden, w_tail[layer_num])
    return hidden


def project(features, w_proj):
    normed = norm_rows(features.astype(jnp.float32)).astype(jnp.bfloat16)
    return jnp.dot(normed, w_proj, preferred_element_type=jnp.float32).astype(jnp.bfloat16)


def local(wave, assign, w_first, w_mid, w_tail, w_proj, centroids, prior):
    samples = wave[0]
    tail_part = passed_along(samples[:HALO], "tm", -1)
    features = encode(jnp.concatenate([samples, tail_part]), w_first, w_mid, w_tail)
    own_labels = assign[0]
    shard_len = centroids.shape[0]
    feat_width = centroids.shape[1]
    first_id = lax.axis_index("tm") * shard_len
    centroid_ids = first_id + jnp.arange(shard_len, dtype=jnp.int32)
    rounded = lax.optimization_barrier(centroids.astype(jnp.bfloat16))
    widened = rounded.astype(jnp.float32)
    centroid_sq = jnp.sum(widened * widened, axis=1)
    frames = project(features, w_proj)
    accumulate_frames = lax.all_gather(frames, "tm", axis=0, tiled=True)
    labels = lax.all_gather(own_labels, "tm", axis=0, tiled=True)
    one_hot = labels[None, :] == centroid_ids[:, None]
    hot_rows = labels[:, None] == centroid_ids[None, :]
    hot_sums = jnp.dot(
        one_hot.astype(jnp.bfloat16), accumulate_frames, preferred_element_type=jnp.float32
    )
    counts = jnp.sum(one_hot.astype(jnp.float32), axis=1)
    products = jnp.einsum(
        "rd,kd->rk", accumulate_frames, rounded, preferred_element_type=jnp.float32
    )
    frame_wide = accumulate_frames.astype(jnp.float32)
    squares = jnp.sum(frame_wide * frame_wide, axis=1)
    is_owner = (labels >= first_id) & (labels < first_id + shard_len)
    picked = jnp.sum(jnp.where(hot_rows, centroid_sq[None, :] - 2.0 * products, 0.0), axis=1)
    own_term = jnp.where(is_owner, squares + picked, 0.0)
    term_sums = lax.psum_scatter(own_term, "tm", scatter_dimension=0, tiled=True)
    distortion = (term_sums / feat_width)[None, :]
    total_sums, total_counts = (
        lax.psum(hot_sums.astype(jnp.bfloat16), "grp").astype(jnp.float32),
        lax.psum(counts.astype(jnp.bfloat16), "grp").astype(jnp.float32),
    )
    new_counts = prior + total_counts
    new_centroids = (prior[:, None] * centroids + total_sums) / new_counts[:, None]
    return (new_centroids, new_counts, distortion)


def solution(mesh):
    return jax.shard_map(
        local,
        mesh=mesh,
        in_specs=(P("grp", "tm"), P("grp", "tm"), P(), P(), P(), P(), P("tm", None), P("tm")),
        out_specs=(P("tm", None), P("tm"), P("grp", "tm")),
        check_vma=False,
    )
```

profile of v0, /device:TPU:0, one launch (start us, length us, event | category | flops | bytes accessed | tf_op | source)
XLA Modules:
  0.0 410.5 jit_solution(17534476603627418723)
XLA Ops:
  14.4 4.5 %slice.152 = bf16[8207,5]{1,0:T(8,128)(2,1)S(1)} reshape(bf16[41035]{0:T(1024)(128)(2,1)S(1)} %get-tuple-element.8) | data formatting | bytes 164140 | tf_op jit(solution)/shard_map/slice | solution.py:30
  19.0 5.9 %slice.149 = bf16[8207,5]{1,0:T(8,128)(2,1)} reshape(bf16[41035]{0:T(1024)(128)(2,1)S(1)} %get-tuple-element.7) | data formatting | bytes 164140 | tf_op jit(solution)/shard_map/slice | solution.py:29
  24.8 8.0 %fusion.115 = f32[8207,512]{1,0:T(8,128)} fusion(bf16[8207,5]{1,0:T(8,128)(2,1)S(1)} %slice.152, bf16[10,512]{1,0:T(8,128)(2,1)S(1)} %copy-done.9), kind=kOutput, calls=%fused_computation.204 | convolution fusion | flops 42019840 | bytes 18917376 | tf_op jit(solution)/shard_map/dot_general | solution.py:30
  32.9 10.8 %fusion.121 = (f32[8207]{0:T(1024)S(1)}, f32[8207,512]{1,0:T(8,128)}) fusion(f32[8207,512]{1,0:T(8,128)} %fusion.115, bf16[8207,5]{1,0:T(8,128)(2,1)S(1)} %copy-done.5, bf16[10,512]{1,0:T(8,128)(2,1)S(1)} %copy-done.9), kind=kOutput, calls=%fused_computation.223 | convolution fusion | flops 50415600 | bytes 35758140 | tf_op jit(solution)/shard_map/dot_general | solution.py:29
  43.7 10.4 %multiply_reduce_fusion = f32[8207]{0:T(1024)S(1)} fusion(f32[8207,512]{1,0:T(8,128)} %get-tuple-element.10, f32[8207]{0:T(1024)S(1)} %broadcast_multiply_fusion), kind=kLoop, calls=%fused_computation.17 | loop fusion | flops 12597745 | bytes 16873592 | tf_op jit(solution)/shard_map/reduce_sum | solution.py:19
  54.4 45.7 %fusion.2 = bf16[8207,512]{1,0:T(8,128)(2,1)} fusion(f32[8207,512]{1,0:T(8,128)S(1)} %copy-done.1, f32[8207]{0:T(1024)S(1)} %add_rsqrt_fusion, f32[8207]{0:T(1024)S(1)} %broadcast_multiply_fusion), kind=kLoop, calls=%fused_computation.3 | loop fusion | flops 281532928 | bytes 25277560 | tf_op jit(solution)/shard_map/convert_element_type | solution.py:24
  100.1 13.0 %slice.155 = bf16[4103,1024]{1,0:T(8,128)(2,1)} reshape(bf16[8206,512]{1,0:T(8,128)(2,1)} %bitcast.63) | data formatting | bytes 16805888 | tf_op jit(solution)/shard_map/slice | solution.py:40
  113.1 8.0 %concatenate.16 = bf16[8208,512]{1,0:T(8,128)(2,1)} pad(bf16[8207,512]{1,0:T(8,128)(2,1)} %fusion.2, bf16[]{:T(256)} %constant.70.clone.1), padding=0_1x0_0 | pad | bytes 16808962 | tf_op jit(solution)/shard_map/concatenate | solution.py:37
  121.1 13.0 %reshape.165 = bf16[4104,1024]{1,0:T(8,128)(2,1)} reshape(bf16[8208,512]{1,0:T(8,128)(2,1)} %concatenate.16) | data formatting | bytes 16809984 | tf_op jit(solution)/shard_map/reshape | solution.py:37
  134.1 7.4 %fusion.64 = f32[4103,512]{1,0:T(8,128)S(1)} fusion(bf16[4103,1024]{1,0:T(8,128)(2,1)} %slice.155, bf16[4,1536,512]{2,1,0:T(8,128)(2,1)} %param.11), kind=kOutput, calls=%fused_computation.114 | convolution fusion | flops 4302307328 | bytes 17856512 | tf_op jit(solution)/shard_map/dot_general | solution.py:40
  147.0 22.3 %fusion.14 = bf16[4103,512]{1,0:T(8,128)(2,1)S(1)} fusion(f32[4103,512]{1,0:T(8,128)S(1)} %get-tuple-element.12, f32[4103]{0:T(1024)S(1)} %add_rsqrt_fusion.1, f32[4103]{0:T(1024)S(1)} %broadcast_multiply_fusion.1), kind=kLoop, calls=%fused_computation.27 | loop fusion | flops 140749312 | bytes 12637240 | tf_op jit(solution)/shard_map/convert_element_type | solution.py:24
  173.6 7.2 %slice.162 = bf16[2051,1024]{1,0:T(8,128)(2,1)} reshape(bf16[4102,512]{1,0:T(8,128)(2,1)} %bitcast.64) | data formatting | bytes 8400896 | tf_op jit(solution)/shard_map/slice | solution.py:40
  180.7 6.8 %fusion.62 = f32[2051,512]{1,0:T(8,128)} fusion(bf16[2051,1024]{1,0:T(8,128)(2,1)} %slice.162, bf16[4,1536,512]{2,1,0:T(8,128)(2,1)} %param.11), kind=kOutput, calls=%fused_computation.112 | convolution fusion | flops 2150629376 | bytes 9459712 | tf_op jit(solution)/shard_map/dot_general | solution.py:40
  187.5 7.2 %reshape.166 = bf16[2052,1024]{1,0:T(8,128)(2,1)} reshape(bf16[4104,512]{1,0:T(8,128)(2,1)} %concatenate.17) | data formatting | bytes 8404992 | tf_op jit(solution)/shard_map/reshape | solution.py:37
  200.1 11.7 %fusion.25 = bf16[2051,512]{1,0:T(8,128)(2,1)S(1)} fusion(f32[2051,512]{1,0:T(8,128)S(1)} %get-tuple-element.14, f32[2051]{0:T(1024)S(1)} %add_rsqrt_fusion.2, f32[2051]{0:T(1024)S(1)} %broadcast_multiply_fusion.2), kind=kLoop, calls=%fused_computation.53 | loop fusion | flops 70357504 | bytes 6317080 | tf_op jit(solution)/shard_map/convert_element_type | solution.py:24
  215.3 4.6 %fusion.60 = f32[1025,512]{1,0:T(8,128)} fusion(bf16[1025,1024]{1,0:T(8,128)(2,1)} %slice.169, bf16[4,1536,512]{2,1,0:T(8,128)(2,1)} %param.11), kind=kOutput, calls=%fused_computation.110 | convolution fusion | flops 1074790400 | bytes 5261312 | tf_op jit(solution)/shard_map/dot_general | solution.py:40
  225.3 5.7 %fusion.41 = bf16[1025,512]{1,0:T(8,128)(2,1)S(1)} fusion(f32[1025,512]{1,0:T(8,128)S(1)} %get-tuple-element.16, f32[1025]{0:T(1024)S(1)} %add_rsqrt_fusion.3, f32[1025]{0:T(1024)S(1)} %broadcast_multiply_fusion.3), kind=kLoop, calls=%fused_computation.79 | loop fusion | flops 35161600 | bytes 3157000 | tf_op jit(solution)/shard_map/convert_element_type | solution.py:24
  248.3 19.6 %all-gather = s32[1,1024]{1,0:T(1,128)S(1)} all-gather(s32[1,128]{1,0:T(1,128)S(1)} %copy-done.10), channel_id=2, replica_groups=mesh['grp'=4,'tm'=8] {'tm'}, dimensions={1}, use_global_device_ids=true | all-gather | bytes 4608 | tf_op jit(solution)/shard_map/all_gather | solution.py:81
  267.9 26.3 %all-gather.3.cloned.1.call-done = bf16[1024,768]{1,0:T(8,128)(2,1)} async-done(((bf16[128,768]{1,0:T(8,128)(2,1)}), bf16[1024,768]{1,0:T(8,128)(2,1)}) %all-gather.3.cloned.1.call-update) | async-done | bytes 1572880 | tf_op jit(solution)/shard_map/all_gather | solution.py:80
  294.2 6.3 %fusion.36 = bf16[2048,768]{1,0:T(8,128)(2,1)} fusion(bf16[1024,768]{1,0:T(8,128)(2,1)} %all-gather.3.cloned.1.call-done, s32[1024]{0:T(1024)S(1)} %bitcast.66, s32[2048]{0:T(1024)S(1)} %iota_add_fusion), kind=kOutput, calls=%fused_computation.74 | convolution fusion | flops 3224895488 | bytes 4730880 | tf_op jit(solution)/shard_map/dot_general | solution.py:84
  303.0 6.4 %psum.15 = bf16[2048]{0:T(1024)(128)(2,1)S(1)} all-reduce(bf16[2048]{0:T(1024)(128)(2,1)S(1)} %fusion.22), channel_id=1, replica_groups=mesh['grp'=4,'tm'=8] {'grp'}, use_global_device_ids=true, to_apply=%region_18.0 | all-reduce | flops 2048 | bytes 8192 | tf_op jit(solution)/shard_map/psum | solution.py:100
  309.8 58.2 %all-reduce.7.cloned.1.call-done = bf16[2048,768]{1,0:T(8,128)(2,1)} async-done(((bf16[2048,768]{1,0:T(8,128)(2,1)}), bf16[2048,768]{1,0:T(8,128)(2,1)}) %all-reduce.7.cloned.1.call-update) | async-done | bytes 3145744 | tf_op jit(solution)/shard_map/psum | solution.py:99
  368.1 8.7 %fusion.120 = (bf16[2048,768]{1,0:T(8,128)(2,1)S(1)}, f32[2048,768]{1,0:T(8,128)}) fusion(f32[2048,768]{1,0:T(8,128)} %param.14, f32[2048]{0:T(1024)S(1)} %convert_add_fusion, bf16[2048,768]{1,0:T(8,128)(2,1)} %all-reduce.7.cloned.1.call-done, f32[2048]{0:T(1024)S(1)} %copy-done.7), kind=kLoop, calls=%fused_computation.222 | loop fusion | flops 7864320 | bytes 18890752 | tf_op jit(solution)/shard_map/convert_element_type | solution.py:76
  381.5 21.4 %all-reduce.4 = f32[1024]{0:T(1024)S(1)} all-reduce(f32[1024]{0:T(1024)S(1)} %add_select_fusion), channel_id=3, replica_groups=mesh['grp'=4,'tm'=8] {'tm'}, use_global_device_ids=true, to_apply=%region_22.23.clone | all-reduce | flops 1024 | bytes 8192
  (87 shorter events, 56.0 us)
Async XLA Ops:
  7.2 240.1 %copy-start = (bf16[512,768]{1,0:T(8,128)(2,1)S(1)}, bf16[512,768]{1,0:T(8,128)(2,1)}, u32[]{:S(2)}) copy-start(bf16[512,768]{1,0:T(8,128)(2,1)} %param.13) | copy-start | bytes 2359300
  7.2 17.6 %copy-start.9 = (bf16[10,512]{1,0:T(8,128)(2,1)S(1)}, bf16[10,512]{1,0:T(8,128)(2,1)}, u32[]{:S(2)}) copy-start(bf16[10,512]{1,0:T(8,128)(2,1)} %param.10) | copy-start | bytes 30724
  7.2 287.0 %all-gather.3.cloned.1.call-start = ((), (), s32[]{:S(2)}) async-start(), calls=%async_computation | async-start | bytes 1769472 | tf_op jit(solution)/shard_map/all_gather | solution.py:80
  8.0 6.3 %collective-permute-start = (bf16[80]{0:T(256)(128)(2,1)S(1)}, bf16[80]{0:T(256)(128)(2,1)S(1)}, u32[]{:S(2)}, u32[]{:S(2)}) collective-permute-start(bf16[80]{0:T(256)(128)(2,1)S(1)} %slice_bitcast_fusion), channel_id=1, source_target_pairs={{1,0},{2,1},{3,2},{4,3},{5,4},{6,5},{7,6},{9,8},{10,9},{11,10},{12... | collective-permute-start | bytes 488 | tf_op jit(solution)/shard_map/ppermute | solution.py:13
  24.8 8.0 %copy-start.5 = (bf16[8207,5]{1,0:T(8,128)(2,1)S(1)}, bf16[8207,5]{1,0:T(8,128)(2,1)}, u32[]{:S(2)}) copy-start(bf16[8207,5]{1,0:T(8,128)(2,1)} %slice.149) | copy-start | bytes 246214
  43.7 10.7 %copy-start.1 = (f32[8207,512]{1,0:T(8,128)S(1)}, f32[8207,512]{1,0:T(8,128)}, u32[]{:S(2)}) copy-start(f32[8207,512]{1,0:T(8,128)} %get-tuple-element.10) | copy-start | bytes 50423812
  134.1 7.4 %copy-start.3 = (bf16[4104,1024]{1,0:T(8,128)(2,1)S(1)}, bf16[4104,1024]{1,0:T(8,128)(2,1)}, u32[]{:S(2)}) copy-start(bf16[4104,1024]{1,0:T(8,128)(2,1)} %reshape.165) | copy-start | bytes 25214980
  169.4 1.9 copy-start.2
  215.3 4.6 %copy-start.4 = (bf16[2052,512]{1,0:T(8,128)(2,1)S(1)}, bf16[2052,512]{1,0:T(8,128)(2,1)}, u32[]{:S(2)}) copy-start(bf16[2052,512]{1,0:T(8,128)(2,1)} %concatenate.18) | copy-start | bytes 6303748
  241.0 7.3 %copy-start.10 = (s32[1,128]{1,0:T(1,128)S(1)}, s32[1,128]{1,0:T(1,128)}, u32[]{:S(2)}) copy-start(s32[1,128]{1,0:T(1,128)} %param.9) | copy-start | bytes 1540
  248.3 119.8 %all-reduce.7.cloned.1.call-start = ((), (), s32[]{:S(2)}) async-start(), calls=%async_computation.1 | async-start | bytes 6291456 | tf_op jit(solution)/shard_map/psum | solution.py:99
  294.2 6.4 %copy-start.11 = (u32[32]{0:T(128)S(1)}, u32[32]{0:T(128)}, u32[]{:S(2)}) copy-start(u32[32]{0:T(128)} %constant.30) | copy-start | bytes 388
  294.2 15.2 %copy-start.7 = (f32[2048]{0:T(1024)S(1)}, f32[2048]{0:T(1024)}, u32[]{:S(2)}) copy-start(f32[2048]{0:T(1024)} %param.15) | copy-start | bytes 24580
  300.6 8.8 %copy-start.6 = (bf16[1024,768]{1,0:T(8,128)(2,1)S(1)}, bf16[1024,768]{1,0:T(8,128)(2,1)}, u32[]{:S(2)}) copy-start(bf16[1024,768]{1,0:T(8,128)(2,1)} %all-gather.3.cloned.1.call-done) | copy-start | bytes 4718596
  309.4 67.3 %copy-start.8 = (f32[2048]{0:T(1024)}, f32[2048]{0:T(1024)S(1)}, u32[]{:S(2)}) copy-start(f32[2048]{0:T(1024)S(1)} %convert_add_fusion) | copy-start | bytes 24580
Sparse Core Ops, SparseCore 0:
  248.4 45.8 all-gather.2
  300.7 67.2 all-reduce.6
where the time goes:
time: 418 us; the launch traced here: 410 us
  other arithmetic  117 us (28%)
  waiting for transfers between devices  88.3 us (21%)
  local copies, waits for them, and re-layouts  72.2 us (17%)
  matrix products  68.8 us (16%)
  blocking collectives  47.4 us (11%)
  between operations  15.2 us (4%)
    convert_element_type x6, other arithmetic, activate(): return jax.nn.gelu(norm_rows(accum), approximate=False).astype(jnp.bfloat16)  89.3 us
    psum x1, waiting for transfers between devices, local(): lax.psum(hot_sums.astype(jnp.bfloat16), 'grp').astype(jnp.float32)  58.2 us
    all_gather x1, waiting for transfers between devices, local(): accumulate_frames = lax.all_gather(frames, 'tm', axis=0, tiled=True)  26.3 us
    slice x5, local copies, waits for them, and re-layouts, odd_layer(): paired[:out_len]  23.4 us
    reshape x4, local copies, waits for them, and re-layouts, odd_layer(): jnp.concatenate([inputs, jnp.zeros((1, channels), inputs.dtype)], axis=0)  22.5 us
    dot_general x4, matrix products, odd_layer(): jnp.dot(paired[:out_len], weight[:2 * channels], preferred_element_type=j...  22.1 us
    unnamed x1, blocking collectives  21.4 us
    all_gather x1, blocking collectives, local(): labels = lax.all_gather(own_labels, 'tm', axis=0, tiled=True)  19.6 us
  transfers between devices with their start and end apart: 3, of which 3 were waited for; matrix products, arithmetic and copies ran while one was open for 1% of the time, Pallas kernels for 0%

commit v1 on v0

--- a/solution.py
+++ b/solution.py
@@ -77,7 +77,15 @@
     widened = rounded.astype(jnp.float32)
     centroid_sq = jnp.sum(widened * widened, axis=1)
     frames = project(features, w_proj)
-    accumulate_frames = lax.all_gather(frames, "tm", axis=0, tiled=True)
+    ways, here = (lax.axis_size("tm"), lax.axis_index("tm"))
+    grown, reach = (frames, 1)
+    while reach < ways:
+        theirs = lax.ppermute(grown, "tm", [(d, d ^ reach) for d in range(ways)])
+        mine_first = jnp.concatenate([grown, theirs], axis=0)
+        theirs_first = jnp.concatenate([theirs, grown], axis=0)
+        grown = jnp.where(here & reach == 0, mine_first, theirs_first)
+        reach = 2 * reach
+    accumulate_frames = grown
     labels = lax.all_gather(own_labels, "tm", axis=0, tiled=True)
     one_hot = labels[None, :] == centroid_ids[:, None]
     hot_rows = labels[:, None] == centroid_ids[None, :]

time: 418 us -> 432 us (1.033)
  blocking collectives: 47.4 us -> 55.7 us
  starting transfers between devices: 1.36 us -> 8.5 us
    all_gather x1 -> x0, waiting for transfers between devices: 26.3 us -> none  [local(): accumulate_frames = lax.all_gather(frames, 'tm', axis=0, tiled=True)]
    ppermute x0 -> x3, waiting for transfers between devices: none -> 14.5 us  [local(): theirs = lax.ppermute(grown, 'tm', [(d, d ^ reach) for d in range(ways)])]
    psum x1, waiting for transfers between devices: 58.2 us -> 68.5 us  [local(): lax.psum(hot_sums.astype(jnp.bfloat16), 'grp').astype(jnp.float32)]
    all_gather x1, blocking collectives: 19.6 us -> 28.6 us  [local(): labels = lax.all_gather(own_labels, 'tm', axis=0, tiled=True)]
    ppermute x0 -> x3, starting transfers between devices: none -> 7.18 us  [local(): theirs = lax.ppermute(grown, 'tm', [(d, d ^ reach) for d in range(ways)])]
  transfers between devices with their start and end apart: 3 -> 5, of which waited for: 3 -> 5; matrix products, arithmetic and copies ran while one was open for 1% -> 1% of each run, Pallas kernels for 0% -> 0%
where the time goes in v1:
time: 432 us; the launch traced here: 425 us
  other arithmetic  118 us (27%)
  waiting for transfers between devices  86.7 us (20%)
  local copies, waits for them, and re-layouts  72.2 us (17%)
  matrix products  68.4 us (16%)
  blocking collectives  55.7 us (13%)
  between operations  15.3 us (4%)
  starting transfers between devices  8.5 us (2%)
    convert_element_type x6, other arithmetic, activate(): return jax.nn.gelu(norm_rows(accum), approximate=False).astype(jnp.bfloat16)  89.3 us
    psum x1, waiting for transfers between devices, local(): lax.psum(hot_sums.astype(jnp.bfloat16), 'grp').astype(jnp.float32)  68.5 us
    all_gather x1, blocking collectives, local(): labels = lax.all_gather(own_labels, 'tm', axis=0, tiled=True)  28.6 us
    slice x5, local copies, waits for them, and re-layouts, odd_layer(): paired[:out_len]  23.4 us
    reshape x4, local copies, waits for them, and re-layouts, odd_layer(): jnp.concatenate([inputs, jnp.zeros((1, channels), inputs.dtype)], axis=0)  22.5 us
    dot_general x4, matrix products, odd_layer(): jnp.dot(paired[:out_len], weight[:2 * channels], preferred_element_type=j...  22.1 us
    unnamed x1, blocking collectives  21.4 us
    ppermute x3, waiting for transfers between devices, local(): theirs = lax.ppermute(grown, 'tm', [(d, d ^ reach) for d in range(ways)])  14.5 us
  transfers between devices with their start and end apart: 5, of which 5 were waited for; matrix products, arithmetic and copies ran while one was open for 1% of the time, Pallas kernels for 0%

profile of v1, /device:TPU:0, one launch (start us, length us, event | category | flops | bytes accessed | tf_op | source)
XLA Modules:
  0.0 424.7 jit_solution(16789756094517130445)
XLA Ops:
  19.0 5.9 %slice.149 = bf16[8207,5]{1,0:T(8,128)(2,1)} reshape(bf16[41035]{0:T(1024)(128)(2,1)S(1)} %get-tuple-element.7) | data formatting | bytes 164140 | tf_op jit(solution)/shard_map/slice | solution.py:29
  24.8 8.0 %fusion.115 = f32[8207,512]{1,0:T(8,128)} fusion(bf16[8207,5]{1,0:T(8,128)(2,1)S(1)} %slice.152, bf16[10,512]{1,0:T(8,128)(2,1)S(1)} %copy-done.8), kind=kOutput, calls=%fused_computation.207 | convolution fusion | flops 42019840 | bytes 18917376 | tf_op jit(solution)/shard_map/dot_general | solution.py:30
  32.9 10.8 %fusion.121 = (f32[8207]{0:T(1024)S(1)}, f32[8207,512]{1,0:T(8,128)}) fusion(f32[8207,512]{1,0:T(8,128)} %fusion.115, bf16[8207,5]{1,0:T(8,128)(2,1)S(1)} %copy-done.5, bf16[10,512]{1,0:T(8,128)(2,1)S(1)} %copy-done.8), kind=kOutput, calls=%fused_computation.226 | convolution fusion | flops 50415600 | bytes 35758140 | tf_op jit(solution)/shard_map/dot_general | solution.py:29
  43.7 10.4 %multiply_reduce_fusion = f32[8207]{0:T(1024)S(1)} fusion(f32[8207,512]{1,0:T(8,128)} %get-tuple-element.10, f32[8207]{0:T(1024)S(1)} %broadcast_multiply_fusion), kind=kLoop, calls=%fused_computation.17 | loop fusion | flops 12597745 | bytes 16873592 | tf_op jit(solution)/shard_map/reduce_sum | solution.py:19
  54.4 45.7 %fusion.2 = bf16[8207,512]{1,0:T(8,128)(2,1)} fusion(f32[8207,512]{1,0:T(8,128)S(1)} %copy-done.1, f32[8207]{0:T(1024)S(1)} %add_rsqrt_fusion, f32[8207]{0:T(1024)S(1)} %broadcast_multiply_fusion), kind=kLoop, calls=%fused_computation.3 | loop fusion | flops 281532928 | bytes 25277560 | tf_op jit(solution)/shard_map/convert_element_type | solution.py:24
  100.0 13.0 %slice.155 = bf16[4103,1024]{1,0:T(8,128)(2,1)} reshape(bf16[8206,512]{1,0:T(8,128)(2,1)} %bitcast.61) | data formatting | bytes 16805888 | tf_op jit(solution)/shard_map/slice | solution.py:40
  113.1 8.0 %concatenate.34 = bf16[8208,512]{1,0:T(8,128)(2,1)} pad(bf16[8207,512]{1,0:T(8,128)(2,1)} %fusion.2, bf16[]{:T(256)} %constant.78.clone.1), padding=0_1x0_0 | pad | bytes 16808962 | tf_op jit(solution)/shard_map/concatenate | solution.py:37
  121.1 13.0 %reshape.165 = bf16[4104,1024]{1,0:T(8,128)(2,1)} reshape(bf16[8208,512]{1,0:T(8,128)(2,1)} %concatenate.34) | data formatting | bytes 16809984 | tf_op jit(solution)/shard_map/reshape | solution.py:37
  134.1 7.4 %fusion.64 = f32[4103,512]{1,0:T(8,128)S(1)} fusion(bf16[4103,1024]{1,0:T(8,128)(2,1)} %slice.155, bf16[4,1536,512]{2,1,0:T(8,128)(2,1)} %param.11), kind=kOutput, calls=%fused_computation.115 | convolution fusion | flops 4302307328 | bytes 17856512 | tf_op jit(solution)/shard_map/dot_general | solution.py:40
  147.0 22.3 %fusion.14 = bf16[4103,512]{1,0:T(8,128)(2,1)S(1)} fusion(f32[4103,512]{1,0:T(8,128)S(1)} %get-tuple-element.12, f32[4103]{0:T(1024)S(1)} %add_rsqrt_fusion.1, f32[4103]{0:T(1024)S(1)} %broadcast_multiply_fusion.1), kind=kLoop, calls=%fused_computation.27 | loop fusion | flops 140749312 | bytes 12637240 | tf_op jit(solution)/shard_map/convert_element_type | solution.py:24
  173.5 7.2 %slice.162 = bf16[2051,1024]{1,0:T(8,128)(2,1)} reshape(bf16[4102,512]{1,0:T(8,128)(2,1)} %bitcast.62) | data formatting | bytes 8400896 | tf_op jit(solution)/shard_map/slice | solution.py:40
  180.7 6.8 %fusion.62 = f32[2051,512]{1,0:T(8,128)} fusion(bf16[2051,1024]{1,0:T(8,128)(2,1)} %slice.162, bf16[4,1536,512]{2,1,0:T(8,128)(2,1)} %param.11), kind=kOutput, calls=%fused_computation.113 | convolution fusion | flops 2150629376 | bytes 9459712 | tf_op jit(solution)/shard_map/dot_general | solution.py:40
  187.5 7.2 %reshape.166 = bf16[2052,1024]{1,0:T(8,128)(2,1)} reshape(bf16[4104,512]{1,0:T(8,128)(2,1)} %concatenate.35) | data formatting | bytes 8404992 | tf_op jit(solution)/shard_map/reshape | solution.py:37
  200.1 11.7 %fusion.25 = bf16[2051,512]{1,0:T(8,128)(2,1)S(1)} fusion(f32[2051,512]{1,0:T(8,128)S(1)} %get-tuple-element.14, f32[2051]{0:T(1024)S(1)} %add_rsqrt_fusion.2, f32[2051]{0:T(1024)S(1)} %broadcast_multiply_fusion.2), kind=kLoop, calls=%fused_computation.53 | loop fusion | flops 70357504 | bytes 6317080 | tf_op jit(solution)/shard_map/convert_element_type | solution.py:24
  215.2 4.6 %fusion.60 = f32[1025,512]{1,0:T(8,128)} fusion(bf16[1025,1024]{1,0:T(8,128)(2,1)} %slice.169, bf16[4,1536,512]{2,1,0:T(8,128)(2,1)} %param.11), kind=kOutput, calls=%fused_computation.111 | convolution fusion | flops 1074790400 | bytes 5261312 | tf_op jit(solution)/shard_map/dot_general | solution.py:40
  225.3 5.7 %fusion.41 = bf16[1025,512]{1,0:T(8,128)(2,1)S(1)} fusion(f32[1025,512]{1,0:T(8,128)S(1)} %get-tuple-element.16, f32[1025]{0:T(1024)S(1)} %add_rsqrt_fusion.3, f32[1025]{0:T(1024)S(1)} %broadcast_multiply_fusion.3), kind=kLoop, calls=%fused_computation.79 | loop fusion | flops 35161600 | bytes 3157000 | tf_op jit(solution)/shard_map/convert_element_type | solution.py:24
  256.0 7.5 %collective-permute-done.2 = bf16[256,768]{1,0:T(8,128)(2,1)S(1)} collective-permute-done((bf16[256,768]{1,0:T(8,128)(2,1)S(1)}, bf16[256,768]{1,0:T(8,128)(2,1)S(1)}, u32[]{:S(2)}, u32[]{:S(2)}) %collective-permute-start.2) | collective-permute-done | bytes 393248 | tf_op jit(solution)/shard_map/ppermute | solution.py:83
  266.4 28.6 %all-gather = s32[1,1024]{1,0:T(1,128)S(1)} all-gather(s32[1,128]{1,0:T(1,128)S(1)} %copy-done.9), channel_id=2, replica_groups=mesh['grp'=4,'tm'=8] {'tm'}, dimensions={1}, use_global_device_ids=true | all-gather | bytes 4608 | tf_op jit(solution)/shard_map/all_gather | solution.py:89
  298.3 5.5 %fusion.36 = bf16[2048,768]{1,0:T(8,128)(2,1)} fusion(s32[1024]{0:T(1024)S(1)} %bitcast.64, s32[2048]{0:T(1024)S(1)} %iota_add_fusion, bf16[512,768]{1,0:T(8,128)(2,1)S(1)} %collective-permute-done.3, bf16[512,768]{1,0:T(8,128)(2,1)S(1)} %maximum_select_fusion.1, pred[]{:T(512)S(6)} %eq.38), kind=kOutput, calls=%fused_computation.74 | convolution fusion | flops 3231973376 | bytes 4730881 | tf_op jit(solution)/shard_map/dot_general | solution.py:92
  306.1 5.7 %psum.15 = bf16[2048]{0:T(1024)(128)(2,1)S(1)} all-reduce(bf16[2048]{0:T(1024)(128)(2,1)S(1)} %fusion.22), channel_id=1, replica_groups=mesh['grp'=4,'tm'=8] {'grp'}, use_global_device_ids=true, to_apply=%region_18.19 | all-reduce | flops 2048 | bytes 8192 | tf_op jit(solution)/shard_map/psum | solution.py:108
  312.4 68.5 %all-reduce.7.cloned.1.call-done = bf16[2048,768]{1,0:T(8,128)(2,1)} async-done(((bf16[2048,768]{1,0:T(8,128)(2,1)}), bf16[2048,768]{1,0:T(8,128)(2,1)}) %all-reduce.7.cloned.1.call-update) | async-done | bytes 3145744 | tf_op jit(solution)/shard_map/psum | solution.py:107
  380.9 8.9 %fusion.120 = (bf16[2048,768]{1,0:T(8,128)(2,1)S(1)}, f32[2048,768]{1,0:T(8,128)}) fusion(f32[2048,768]{1,0:T(8,128)} %param.14, f32[2048]{0:T(1024)S(1)} %convert_add_fusion, bf16[2048,768]{1,0:T(8,128)(2,1)} %all-reduce.7.cloned.1.call-done, f32[2048]{0:T(1024)S(1)} %copy-done.6), kind=kLoop, calls=%fused_computation.225 | loop fusion | flops 7864320 | bytes 18890752 | tf_op jit(solution)/shard_map/convert_element_type | solution.py:76
  390.5 5.2 %select_reduce_fusion = f32[1024]{0:T(1024)S(1)} fusion(bf16[2048,768]{1,0:T(8,128)(2,1)S(1)} %get-tuple-element.5, f32[2048]{0:T(1024)S(1)} %multiply_reduce_fusion.2, s32[2048]{0:T(1024)S(1)} %iota_add_fusion, s32[1024]{0:T(1024)S(1)} %bitcast.66, bf16[512,768]{1,0:T(8,128)(2,1)S(1)} %collective-permute-done.3, ...), kind=kOutput, calls=%fused_computation.45 | convolution fusion | flops 3238788096 | bytes 4743169 | tf_op jit(solution)/shard_map/rd,kd->rk/dot_general | solution.py:96
  395.7 21.4 %all-reduce.4 = f32[1024]{0:T(1024)S(1)} all-reduce(f32[1024]{0:T(1024)S(1)} %add_select_fusion), channel_id=3, replica_groups=mesh['grp'=4,'tm'=8] {'tm'}, use_global_device_ids=true, to_apply=%region_22.23.clone | all-reduce | flops 1024 | bytes 8192
  (90 shorter events, 70.5 us)
Async XLA Ops:
  7.2 240.0 %copy-start = (bf16[512,768]{1,0:T(8,128)(2,1)S(1)}, bf16[512,768]{1,0:T(8,128)(2,1)}, u32[]{:S(2)}) copy-start(bf16[512,768]{1,0:T(8,128)(2,1)} %param.13) | copy-start | bytes 2359300
  7.2 17.6 %copy-start.8 = (bf16[10,512]{1,0:T(8,128)(2,1)S(1)}, bf16[10,512]{1,0:T(8,128)(2,1)}, u32[]{:S(2)}) copy-start(bf16[10,512]{1,0:T(8,128)(2,1)} %param.10) | copy-start | bytes 30724
  7.2 373.7 %all-reduce.7.cloned.1.call-start = ((), (), s32[]{:S(2)}) async-start(), calls=%async_computation | async-start | bytes 6291456 | tf_op jit(solution)/shard_map/psum | solution.py:107
  8.0 6.3 %collective-permute-start = (bf16[80]{0:T(256)(128)(2,1)S(1)}, bf16[80]{0:T(256)(128)(2,1)S(1)}, u32[]{:S(2)}, u32[]{:S(2)}) collective-permute-start(bf16[80]{0:T(256)(128)(2,1)S(1)} %slice_bitcast_fusion), channel_id=1, source_target_pairs={{1,0},{2,1},{3,2},{4,3},{5,4},{6,5},{7,6},{9,8},{10,9},{11,10},{12... | collective-permute-start | bytes 488 | tf_op jit(solution)/shard_map/ppermute | solution.py:13
  24.8 8.0 %copy-start.5 = (bf16[8207,5]{1,0:T(8,128)(2,1)S(1)}, bf16[8207,5]{1,0:T(8,128)(2,1)}, u32[]{:S(2)}) copy-start(bf16[8207,5]{1,0:T(8,128)(2,1)} %slice.149) | copy-start | bytes 246214
  43.7 10.7 %copy-start.1 = (f32[8207,512]{1,0:T(8,128)S(1)}, f32[8207,512]{1,0:T(8,128)}, u32[]{:S(2)}) copy-start(f32[8207,512]{1,0:T(8,128)} %get-tuple-element.10) | copy-start | bytes 50423812
  134.1 7.4 %copy-start.3 = (bf16[4104,1024]{1,0:T(8,128)(2,1)S(1)}, bf16[4104,1024]{1,0:T(8,128)(2,1)}, u32[]{:S(2)}) copy-start(bf16[4104,1024]{1,0:T(8,128)(2,1)} %reshape.165) | copy-start | bytes 25214980
  169.3 1.9 copy-start.2
  215.2 4.6 %copy-start.4 = (bf16[2052,512]{1,0:T(8,128)(2,1)S(1)}, bf16[2052,512]{1,0:T(8,128)(2,1)}, u32[]{:S(2)}) copy-start(bf16[2052,512]{1,0:T(8,128)(2,1)} %concatenate.36) | copy-start | bytes 6303748
  242.7 23.7 %copy-start.9 = (s32[1,128]{1,0:T(1,128)S(1)}, s32[1,128]{1,0:T(1,128)}, u32[]{:S(2)}) copy-start(s32[1,128]{1,0:T(1,128)} %param.9) | copy-start | bytes 1540
  247.5 6.8 %collective-permute-start.1 = (bf16[128,768]{1,0:T(8,128)(2,1)S(1)}, bf16[128,768]{1,0:T(8,128)(2,1)S(1)}, u32[]{:S(2)}, u32[]{:S(2)}) collective-permute-start(bf16[128,768]{1,0:T(8,128)(2,1)S(1)} %convolution_convert_fusion), channel_id=1, source_target_pairs={{0,1},{1,0},{2,3},{3,2},{4,5},{5,4},{6,7},{7,6},{8,9},{9,8},{10,11... | collective-permute-start | bytes 589832 | tf_op jit(solution)/shard_map/ppermute | solution.py:83
  254.4 9.2 %collective-permute-start.2 = (bf16[256,768]{1,0:T(8,128)(2,1)S(1)}, bf16[256,768]{1,0:T(8,128)(2,1)S(1)}, u32[]{:S(2)}, u32[]{:S(2)}) collective-permute-start(bf16[256,768]{1,0:T(8,128)(2,1)S(1)} %maximum_select_fusion.2), channel_id=1, source_target_pairs={{0,2},{1,3},{2,0},{3,1},{4,6},{5,7},{6,4},{7,5},{8,10},{9,11},{10,... | collective-permute-start | bytes 1179656 | tf_op jit(solution)/shard_map/ppermute | solution.py:83
  263.8 34.4 %collective-permute-start.3 = (bf16[512,768]{1,0:T(8,128)(2,1)S(1)}, bf16[512,768]{1,0:T(8,128)(2,1)S(1)}, u32[]{:S(2)}, u32[]{:S(2)}) collective-permute-start(bf16[512,768]{1,0:T(8,128)(2,1)S(1)} %maximum_select_fusion.1), channel_id=1, source_target_pairs={{0,4},{1,5},{2,6},{3,7},{4,0},{5,1},{6,2},{7,3},{8,12},{9,13},{10,... | collective-permute-start | bytes 2359304 | tf_op jit(solution)/shard_map/ppermute | solution.py:83
  298.3 5.5 %copy-start.10 = (u32[32]{0:T(128)S(1)}, u32[32]{0:T(128)}, u32[]{:S(2)}) copy-start(u32[32]{0:T(128)} %constant.30) | copy-start | bytes 388
  298.3 13.5 %copy-start.6 = (f32[2048]{0:T(1024)S(1)}, f32[2048]{0:T(1024)}, u32[]{:S(2)}) copy-start(f32[2048]{0:T(1024)} %param.15) | copy-start | bytes 24580
  311.8 78.0 %copy-start.7 = (f32[2048]{0:T(1024)}, f32[2048]{0:T(1024)S(1)}, u32[]{:S(2)}) copy-start(f32[2048]{0:T(1024)S(1)} %convert_add_fusion) | copy-start | bytes 24580
Sparse Core Ops, SparseCore 0:
  303.9 76.9 all-reduce.6
